TPU v7x, 256 devices: a whole 4x4x8 slice. The times are simulated.
256 devices in a mesh: buoy: 4 (over x), dom: 64 (over z, y, core).
Axes of the slice: x: 4, y: 4, z: 8, core: 2. Of those that a mesh axis runs over, the one named last changes fastest.
Arguments:
- ambient: float32 [32, 36, 448], P('buoy', None, 'dom'), may hold values from -6 to 6
- initial_out: float32 [32, 36, 448], P('buoy', None, 'dom'), may hold values from -6 to 6
- translation: bfloat16 [512, 448, 448], P(('buoy', 'dom')), may hold values from -0.0625 to 0.0625
- pair_source: int32 [512], P(('buoy', 'dom')), may hold values from 0 to 31, as said below
- pair_target: int32 [512], P(('buoy', 'dom')), may hold values from 0 to 31, as said below
- pair_live: int32 [512], P(('buoy', 'dom')), may hold values from 0 to 1, as said below
- diffract: bfloat16 [448, 448], P('dom'), may hold values from -0.25 to 0.25
- panel_rows: bfloat16 [8192, 448], P('dom'), may hold values from -0.25 to 0.25
Outputs:
- outgoing: float32 [32, 36, 448], P('buoy', None, 'dom')
- sources: bfloat16 [32, 36, 8192], P('buoy', None, 'dom')
Inputs may be any that keep to these rules, and one draw needn't show every extreme that they name: `pair_target`: the slots of one device name target buoys among the 8 buoys of its index of buoy. `pair_source`: A source buoy differs from its target by 1 to 8 places in the farm's order; the live slots of one target name distinct sources. `pair_live`: A slot is live exactly where its source lies inside the farm; some device has all 2 live.
All inputs are finite; a program needn't handle non-finite values.
Results may differ from a plain program's by a relative error of at most 0.015.
Values may be sent and summed in bfloat16 or wider, within the bound.
No kernel may reach another device: no remote copies, remote signals or barrier semaphores. Data moves between devices by JAX's collectives and lax.ppermute only.
A program may use at most 64 MiB of HBM per device.

v0:
```python
import jax
import jax.numpy as jnp
from jax import lax
from jax.sharding import PartitionSpec as P

ITERS = 2


def extended_2(block, sides, width):
    for axis, dim in sides:
        count = lax.axis_size(axis)
        forward = [(i, i + 1) for i in range(count - 1)]
        backward = [(target, source) for source, target in forward]
        low = lax.ppermute(
            lax.slice_in_dim(block, block.shape[dim] - width, None, axis=dim), axis, forward
        )
        high = lax.ppermute(lax.slice_in_dim(block, 0, width, axis=dim), axis, backward)
        block = jnp.concatenate([low, block, high], axis=dim)
    return block


def rows_product(left, right):
    return lax.dot_general(
        left, right, (((1,), (1,)), ((), ())), preferred_element_type=jnp.float32
    )


def shards(
    ambient, initial_out, translation, pair_source, pair_target, pair_live, diffract, panel_rows
):
    per_dev, headings, share_width = initial_out.shape
    full_width = translation.shape[1]
    first_buoy = lax.axis_index("buoy") * per_dev
    column_start = lax.axis_index("dom") * share_width
    rows_source = pair_source - (first_buoy - per_dev)
    rows_target = pair_target - first_buoy
    place_table = (
        (rows_target[None, :] == jnp.arange(per_dev, dtype=jnp.int32)[:, None])
        & (pair_live[None, :] == 1)
    ).astype(jnp.float32)
    matrices = translation.astype(jnp.float32)
    coeffs = initial_out
    incident_bf = None
    for step in range(ITERS):
        whole = lax.all_gather(coeffs, "dom", axis=2, tiled=True)
        extended = extended_2(whole.astype(jnp.bfloat16), (("buoy", 0),), per_dev).astype(
            whole.dtype
        )
        picked = jnp.take(extended, rows_source, axis=0)
        terms = jnp.einsum("phn,pmn->phm", picked, matrices, precision=lax.Precision.HIGHEST)
        partial_value = jnp.einsum(
            "kp,phm->khm", place_table, terms, precision=lax.Precision.HIGHEST
        )
        own_columns = (
            lax.dynamic_slice_in_dim(partial_value, column_start, share_width, 2) + ambient
        )
        partial_value = lax.dynamic_update_slice_in_dim(partial_value, own_columns, column_start, 2)
        incident = lax.psum(partial_value, "dom")
        incident_bf = incident.astype(jnp.bfloat16)
        flat = incident_bf.reshape(per_dev * headings, full_width)
        coeffs = rows_product(flat, diffract).reshape(per_dev, headings, share_width)
    flat = incident_bf.reshape(per_dev * headings, full_width)
    sources = (
        rows_product(flat, panel_rows)
        .astype(jnp.bfloat16)
        .reshape(per_dev, headings, panel_rows.shape[0])
    )
    return (coeffs, sources)


def solution(mesh):
    in_specs = (
        P("buoy", None, "dom"),
        P("buoy", None, "dom"),
        P(("buoy", "dom"), None, None),
        P(("buoy", "dom")),
        P(("buoy", "dom")),
        P(("buoy", "dom")),
        P("dom", None),
        P("dom", None),
    )
    out_specs = (P("buoy", None, "dom"), P("buoy", None, "dom"))
    return jax.shard_map(shards, mesh=mesh, in_specs=in_specs, out_specs=out_specs, check_vma=False)
```

profile of v0, /device:TPU:6, one launch (start us, length us, event | category | flops | bytes accessed | tf_op | source)
XLA Modules:
  0.0 659.2 jit_solution(17983448239093237719)
XLA Ops:
  0.7 0.8 convert.2
  1.5 53.9 %all_gather.6 = bf16[8,36,448]{1,0,2:T(8,128)(2,1)S(1)} all-gather(bf16[8,36,7]{1,0,2:T(8,128)(2,1)S(1)} %convert.2), channel_id=1, replica_groups=mesh['buoy'=4,'dom'=64] {'dom'}, dimensions={2}, use_global_device_ids=true | all-gather | bytes 262080 | tf_op jit(solution)/shard_map/all_gather | solution.py:45
  55.4 0.7 copy.70
  56.1 2.7 collective-permute-start.1
  58.9 1.3 collective-permute-start
  60.4 5.9 collective-permute-done.1
  66.3 0.7 copy-done.1
  67.0 3.5 collective-permute-done
  70.6 1.3 maximum_convert_fusion
  71.8 0.6 gather_fusion
  72.4 0.9 fusion.4
  73.3 0.6 fusion.8
  74.0 0.6 dynamic_update_slice.6
  74.6 258.2 %all-reduce.2 = bf16[8,36,448]{2,0,1:T(8,128)(2,1)S(1)} all-reduce(f32[8,36,448]{2,0,1:T(8,128)S(1)} %dynamic_update_slice.6), channel_id=1, replica_groups=mesh['buoy'=4,'dom'=64] {'dom'}, use_global_device_ids=true, to_apply=%region_0.0 | all-reduce | flops 129024 | bytes 774144 | tf_op jit(solution)/shard_map/psum | solution.py:58
  332.9 0.3 fusion
  333.2 47.3 %all_gather.7 = bf16[8,36,448]{1,0,2:T(8,128)(2,1)S(1)} all-gather(bf16[8,36,7]{1,0,2:T(8,128)(2,1)S(1)} %copy.74), channel_id=1, replica_groups=mesh['buoy'=4,'dom'=64] {'dom'}, dimensions={2}, use_global_device_ids=true | all-gather | bytes 262080 | tf_op jit(solution)/shard_map/all_gather | solution.py:45
  380.5 0.9 copy.75
  381.4 2.4 collective-permute-start.3
  383.9 1.5 collective-permute-start.2
  385.3 5.3 collective-permute-done.3
  390.6 4.1 collective-permute-done.2
  394.7 0.2 maximum_convert_fusion.1
  395.0 1.0 copy.76
  396.0 0.6 gather_fusion.1
  396.6 0.9 fusion.2
  397.5 0.6 fusion.6
  398.2 0.6 dynamic_update_slice.7
  398.8 258.3 %all-reduce.3 = bf16[8,36,448]{2,0,1:T(8,128)(2,1)S(1)} all-reduce(f32[8,36,448]{2,0,1:T(8,128)S(1)} %dynamic_update_slice.7), channel_id=1, replica_groups=mesh['buoy'=4,'dom'=64] {'dom'}, use_global_device_ids=true, to_apply=%region_1.3 | all-reduce | flops 129024 | bytes 774144 | tf_op jit(solution)/shard_map/psum | solution.py:58
  657.1 0.3 fusion.14
  657.5 0.6 copy.81
  658.2 0.2 convolution_convert_fusion
  658.5 0.6 copy.82
  (26 shorter events, 0.7 us)
Async XLA Ops:
  0.6 71.8 %copy-start = (bf16[2,448,448]{2,1,0:T(8,128)(2,1)S(1)}, bf16[2,448,448]{2,1,0:T(8,128)(2,1)}, u32[]{:S(2)}) copy-start(bf16[2,448,448]{2,1,0:T(8,128)(2,1)} %param.12) | copy-start | bytes 2408452
  0.6 59.5 %copy-start.6 = (s32[2]{0:T(128)S(1)}, s32[2]{0:T(128)}, u32[]{:S(2)}) copy-start(s32[2]{0:T(128)} %param.14) | copy-start | bytes 28
  0.7 59.5 %copy-start.4 = (s32[2]{0:T(128)S(1)}, s32[2]{0:T(128)}, u32[]{:S(2)}) copy-start(s32[2]{0:T(128)} %param.13) | copy-start | bytes 28
  0.7 59.6 %copy-start.3 = (f32[8,36,7]{1,0,2:T(8,128)S(1)}, f32[8,36,7]{1,0,2:T(8,128)}, u32[]{:S(2)}) copy-start(f32[8,36,7]{1,0,2:T(8,128)} %param.10) | copy-start | bytes 24196
  0.7 59.7 %copy-start.7 = (s32[2]{0:T(128)S(1)}, s32[2]{0:T(128)}, u32[]{:S(2)}) copy-start(s32[2]{0:T(128)} %param.15) | copy-start | bytes 28
  56.1 10.2 %collective-permute-start.1 = (bf16[8,36,448]{2,1,0:T(8,128)(2,1)S(1)}, bf16[8,36,448]{2,1,0:T(8,128)(2,1)S(1)}, u32[]{:S(2)}, u32[]{:S(2)}) collective-permute-start(bf16[8,36,448]{2,1,0:T(8,128)(2,1)S(1)} %copy.70), channel_id=1, source_target_pairs={{64,0},{128,64},{192,128},{65,1},{129,65},{193,129},{66,2},{130,66... | collective-permute-start | bytes 774152 | tf_op jit(solution)/shard_map/ppermute | solution.py:17
  58.9 11.7 %collective-permute-start = (bf16[8,36,448]{2,1,0:T(8,128)(2,1)S(1)}, bf16[8,36,448]{2,1,0:T(8,128)(2,1)}, u32[]{:S(2)}, u32[]{:S(2)}) collective-permute-start(bf16[8,36,448]{2,1,0:T(8,128)(2,1)S(1)} %copy.70), channel_id=1, source_target_pairs={{0,64},{64,128},{128,192},{1,65},{65,129},{129,193},{2,66},{66,130... | collective-permute-start | bytes 774152 | tf_op jit(solution)/shard_map/ppermute | solution.py:14
  66.3 0.7 copy-start.1
  72.4 260.5 %copy-start.5 = (bf16[7,448]{1,0:T(8,128)(2,1)S(1)}, bf16[7,448]{1,0:T(8,128)(2,1)}, u32[]{:S(2)}) copy-start(bf16[7,448]{1,0:T(8,128)(2,1)} %param.16) | copy-start | bytes 18820
  381.4 9.2 %collective-permute-start.3 = (bf16[8,36,448]{2,0,1:T(8,128)(2,1)S(1)}, bf16[8,36,448]{2,0,1:T(8,128)(2,1)S(1)}, u32[]{:S(2)}, u32[]{:S(2)}) collective-permute-start(bf16[8,36,448]{2,0,1:T(8,128)(2,1)S(1)} %copy.75), channel_id=1, source_target_pairs={{64,0},{128,64},{192,128},{65,1},{129,65},{193,129},{66,2},{130,66... | collective-permute-start | bytes 774152 | tf_op jit(solution)/shard_map/ppermute | solution.py:17
  383.9 10.9 %collective-permute-start.2 = (bf16[8,36,448]{2,0,1:T(8,128)(2,1)S(1)}, bf16[8,36,448]{2,0,1:T(8,128)(2,1)S(1)}, u32[]{:S(2)}, u32[]{:S(2)}) collective-permute-start(bf16[8,36,448]{2,0,1:T(8,128)(2,1)S(1)} %copy.75), channel_id=1, source_target_pairs={{0,64},{64,128},{128,192},{1,65},{65,129},{129,193},{2,66},{66,130... | collective-permute-start | bytes 774152 | tf_op jit(solution)/shard_map/ppermute | solution.py:14
  398.1 260.2 %copy-start.2 = (bf16[128,448]{0,1:T(8,128)(2,1)S(1)}, bf16[128,448]{0,1:T(8,128)(2,1)}, u32[]{:S(2)}) copy-start(bf16[128,448]{0,1:T(8,128)(2,1)} %param.17) | copy-start | bytes 344068
where the time goes:
time: 659 us
  blocking collectives  618 us (94%)
  waiting for transfers between devices  18.8 us (3%)
  starting transfers between devices  7.95 us (1%)
  local copies, waits for them, and re-layouts  7.34 us (1%)
    psum x2, blocking collectives, shards(): incident = lax.psum(partial_value, 'dom')  517 us
    all_gather x2, blocking collectives, shards(): whole = lax.all_gather(coeffs, 'dom', axis=2, tiled=True)  101 us
  transfers between devices with their start and end apart: 4, of which 4 were waited for; matrix products, arithmetic and copies ran while one was open for 0% of the time, Pallas kernels for 0%

commit v1 on v0

--- a/solution.py
+++ b/solution.py
@@ -42,7 +42,9 @@
     coeffs = initial_out
     incident_bf = None
     for step in range(ITERS):
-        whole = lax.all_gather(coeffs, "dom", axis=2, tiled=True)
+        whole = jnp.concatenate(
+            lax.all_to_all(jnp.stack([coeffs] * lax.axis_size("dom"), 0), "dom", 0, 0), 2
+        )
         extended = extended_2(whole.astype(jnp.bfloat16), (("buoy", 0),), per_dev).astype(
             whole.dtype
         )

time: 659 us -> 602 us (0.914)
  blocking collectives: 618 us -> 531 us
  waiting for transfers between devices: 18.8 us -> 32.3 us
  starting transfers between devices: 7.95 us -> 20.1 us
    all_gather x2 -> x0, blocking collectives: 101 us -> none  [shards(): whole = lax.all_gather(coeffs, 'dom', axis=2, tiled=True)]
    all_to_all x0 -> x1, blocking collectives: none -> 16.7 us  [shards(): lax.all_to_all(jnp.stack([coeffs] * lax.axis_size('dom'), 0), 'dom', 0, 0)]
    all_to_all x0 -> x1, waiting for transfers between devices: none -> 12.9 us  [shards(): lax.all_to_all(jnp.stack([coeffs] * lax.axis_size('dom'), 0), 'dom', 0, 0)]
    all_to_all x0 -> x1, starting transfers between devices: none -> 12.1 us  [shards(): lax.all_to_all(jnp.stack([coeffs] * lax.axis_size('dom'), 0), 'dom', 0, 0)]
  transfers between devices with their start and end apart: 4 -> 5, of which waited for: 4 -> 5; matrix products, arithmetic and copies ran while one was open for 0% -> 0% of each run, Pallas kernels for 0% -> 0%
where the time goes in v1:
time: 602 us; the launch traced here: 601 us
  blocking collectives  531 us (88%)
  waiting for transfers between devices  32.3 us (5%)
  starting transfers between devices  20.1 us (3%)
  local copies, waits for them, and re-layouts  11.4 us (2%)
    psum x2, blocking collectives, shards(): incident = lax.psum(partial_value, 'dom')  514 us
    all_to_all x1, blocking collectives, shards(): lax.all_to_all(jnp.stack([coeffs] * lax.axis_size('dom'), 0), 'dom', 0, 0)  16.7 us
    all_to_all x1, waiting for transfers between devices, shards(): lax.all_to_all(jnp.stack([coeffs] * lax.axis_size('dom'), 0), 'dom', 0, 0)  12.9 us
    all_to_all x1, starting transfers between devices, shards(): lax.all_to_all(jnp.stack([coeffs] * lax.axis_size('dom'), 0), 'dom', 0, 0)  12.1 us
  transfers between devices with their start and end apart: 5, of which 5 were waited for; matrix products, arithmetic and copies ran while one was open for 0% of the time, Pallas kernels for 0%

profile of v1, /device:TPU:6, one launch (start us, length us, event | category | flops | bytes accessed | tf_op | source)
XLA Modules:
  0.0 601.2 jit_solution(17534069284994556316)
XLA Ops:
  0.7 0.9 broadcast_bitcast_fusion.1
  1.6 1.5 reshape.64
  3.1 12.1 %all-to-all-start = ((bf16[64,2,1008]{2,1,0:T(2,128)(2,1)}), bf16[64,2,1008]{2,1,0:T(2,128)(2,1)S(1)}, u32[]{:S(2)}, u32[]{:S(2)}) async-start(bf16[64,2,1008]{2,1,0:T(2,128)(2,1)} %reshape.64), calls=%async_computation | async-start | bytes 524288 | tf_op jit(solution)/shard_map/all_to_all | solution.py:46
  15.3 12.9 %all-to-all-done = bf16[64,2,1008]{2,1,0:T(2,128)(2,1)S(1)} async-done(((bf16[64,2,1008]{2,1,0:T(2,128)(2,1)}), bf16[64,2,1008]{2,1,0:T(2,128)(2,1)S(1)}, u32[]{:S(2)}, u32[]{:S(2)}) %all-to-all-start) | async-done | bytes 258080 | tf_op jit(solution)/shard_map/all_to_all | solution.py:46
  28.2 1.0 reshape.65
  29.2 0.7 copy.26
  29.9 2.7 collective-permute-start.1
  32.6 1.3 collective-permute-start
  34.2 5.8 collective-permute-done.1
  40.0 0.7 copy-done.1
  40.7 3.5 collective-permute-done
  44.2 1.3 maximum_convert_fusion
  45.5 0.6 gather_fusion
  46.1 0.9 fusion.4
  47.0 0.6 fusion.8
  47.7 0.6 dynamic_update_slice.6
  48.3 257.1 %all-reduce.2 = bf16[8,36,448]{2,0,1:T(8,128)(2,1)S(1)} all-reduce(f32[8,36,448]{2,0,1:T(8,128)S(1)} %dynamic_update_slice.6), channel_id=1, replica_groups=mesh['buoy'=4,'dom'=64] {'dom'}, use_global_device_ids=true, to_apply=%region_0.0 | all-reduce | flops 129024 | bytes 774144 | tf_op jit(solution)/shard_map/psum | solution.py:60
  305.9 0.8 reshape.66
  306.7 16.7 %all_to_all.10 = bf16[64,2,1008]{2,1,0:T(2,128)(2,1)S(1)} all-to-all(bf16[64,2,1008]{2,1,0:T(2,128)(2,1)S(1)} %reshape.66), channel_id=1, replica_groups=mesh['buoy'=4,'dom'=64] {'dom'}, dimensions={0} | all-to-all | bytes 516096 | tf_op jit(solution)/shard_map/all_to_all | solution.py:46
  323.4 1.0 reshape.67
  324.4 0.7 copy.33
  325.1 2.5 collective-permute-start.3
  327.6 1.5 collective-permute-start.2
  329.0 5.9 collective-permute-done.3
  334.9 4.1 collective-permute-done.2
  339.2 0.6 gather_fusion.1
  339.8 0.9 fusion.2
  340.7 0.6 fusion.6
  341.4 0.6 dynamic_update_slice.7
  342.0 257.1 %all-reduce.3 = bf16[8,36,448]{2,0,1:T(8,128)(2,1)S(1)} all-reduce(f32[8,36,448]{2,0,1:T(8,128)S(1)} %dynamic_update_slice.7), channel_id=1, replica_groups=mesh['buoy'=4,'dom'=64] {'dom'}, use_global_device_ids=true, to_apply=%region_1.3 | all-reduce | flops 129024 | bytes 774144 | tf_op jit(solution)/shard_map/psum | solution.py:60
  599.5 0.6 copy.40
  600.5 0.6 copy.41
  (31 shorter events, 1.8 us)
Async XLA Ops:
  0.6 45.5 %copy-start = (bf16[2,448,448]{2,1,0:T(8,128)(2,1)S(1)}, bf16[2,448,448]{2,1,0:T(8,128)(2,1)}, u32[]{:S(2)}) copy-start(bf16[2,448,448]{2,1,0:T(8,128)(2,1)} %param.12) | copy-start | bytes 2408452
  0.6 14.6 %copy-start.6 = (s32[2]{0:T(128)S(1)}, s32[2]{0:T(128)}, u32[]{:S(2)}) copy-start(s32[2]{0:T(128)} %param.14) | copy-start | bytes 28
  0.7 14.6 %copy-start.4 = (s32[2]{0:T(128)S(1)}, s32[2]{0:T(128)}, u32[]{:S(2)}) copy-start(s32[2]{0:T(128)} %param.13) | copy-start | bytes 28
  1.6 32.4 %copy-start.3 = (f32[8,36,7]{1,0,2:T(8,128)S(1)}, f32[8,36,7]{1,0,2:T(8,128)}, u32[]{:S(2)}) copy-start(f32[8,36,7]{1,0,2:T(8,128)} %param.10) | copy-start | bytes 24196
  1.6 32.5 %copy-start.7 = (s32[2]{0:T(128)S(1)}, s32[2]{0:T(128)}, u32[]{:S(2)}) copy-start(s32[2]{0:T(128)} %param.15) | copy-start | bytes 28
  3.1 25.1 %all-to-all-start = ((bf16[64,2,1008]{2,1,0:T(2,128)(2,1)}), bf16[64,2,1008]{2,1,0:T(2,128)(2,1)S(1)}, u32[]{:S(2)}, u32[]{:S(2)}) async-start(bf16[64,2,1008]{2,1,0:T(2,128)(2,1)} %reshape.64), calls=%async_computation | async-start | bytes 524288 | tf_op jit(solution)/shard_map/all_to_all | solution.py:46
  29.9 10.1 %collective-permute-start.1 = (bf16[8,36,448]{2,1,0:T(8,128)(2,1)S(1)}, bf16[8,36,448]{2,1,0:T(8,128)(2,1)S(1)}, u32[]{:S(2)}, u32[]{:S(2)}) collective-permute-start(bf16[8,36,448]{2,1,0:T(8,128)(2,1)S(1)} %copy.26), channel_id=1, source_target_pairs={{64,0},{128,64},{192,128},{65,1},{129,65},{193,129},{66,2},{130,66... | collective-permute-start | bytes 774152 | tf_op jit(solution)/shard_map/ppermute | solution.py:17
  32.6 11.6 %collective-permute-start = (bf16[8,36,448]{2,1,0:T(8,128)(2,1)S(1)}, bf16[8,36,448]{2,1,0:T(8,128)(2,1)}, u32[]{:S(2)}, u32[]{:S(2)}) collective-permute-start(bf16[8,36,448]{2,1,0:T(8,128)(2,1)S(1)} %copy.26), channel_id=1, source_target_pairs={{0,64},{64,128},{128,192},{1,65},{65,129},{129,193},{2,66},{66,130... | collective-permute-start | bytes 774152 | tf_op jit(solution)/shard_map/ppermute | solution.py:14
  40.0 0.7 copy-start.1
  45.5 259.9 %copy-start.5 = (bf16[7,448]{1,0:T(8,128)(2,1)S(1)}, bf16[7,448]{1,0:T(8,128)(2,1)}, u32[]{:S(2)}) copy-start(bf16[7,448]{1,0:T(8,128)(2,1)} %param.16) | copy-start | bytes 18820
  325.1 9.8 %collective-permute-start.3 = (bf16[8,36,448]{2,1,0:T(8,128)(2,1)S(1)}, bf16[8,36,448]{2,1,0:T(8,128)(2,1)S(1)}, u32[]{:S(2)}, u32[]{:S(2)}) collective-permute-start(bf16[8,36,448]{2,1,0:T(8,128)(2,1)S(1)} %copy.33), channel_id=1, source_target_pairs={{64,0},{128,64},{192,128},{65,1},{129,65},{193,129},{66,2},{130,66... | collective-permute-start | bytes 774152 | tf_op jit(solution)/shard_map/ppermute | solution.py:17
  327.6 11.5 %collective-permute-start.2 = (bf16[8,36,448]{2,1,0:T(8,128)(2,1)S(1)}, bf16[8,36,448]{2,1,0:T(8,128)(2,1)S(1)}, u32[]{:S(2)}, u32[]{:S(2)}) collective-permute-start(bf16[8,36,448]{2,1,0:T(8,128)(2,1)S(1)} %copy.33), channel_id=1, source_target_pairs={{0,64},{64,128},{128,192},{1,65},{65,129},{129,193},{2,66},{66,130... | collective-permute-start | bytes 774152 | tf_op jit(solution)/shard_map/ppermute | solution.py:14
  340.7 259.5 %copy-start.2 = (bf16[128,448]{0,1:T(8,128)(2,1)S(1)}, bf16[128,448]{0,1:T(8,128)(2,1)}, u32[]{:S(2)}) copy-start(bf16[128,448]{0,1:T(8,128)(2,1)} %param.17) | copy-start | bytes 344068
